TPU v7x, 512 devices: a whole 4x8x8 slice. The times are simulated.
512 devices in a mesh: lon: 16 (over z_hi, x, core), lat: 32 (over z_lo, y).
Axes of the slice: x: 4, y: 8, z: 8 (z_hi: 2, z_lo: 4; z = z_hi * 4 + z_lo), core: 2. Of those that a mesh axis runs over, the one named last changes fastest.
Arguments:
- model_state: float32 [4, 8, 1024, 5760], P(None, None, 'lat', 'lon')
- courant: float32 [1024], P('lat'), may hold values from 0.02 to 0.08
- cutoff: int32 [1024], replicated, may hold values from 1 to 2880, as said below
Outputs:
- new_state: float32 [4, 8, 1024, 5760], P(None, None, 'lat', 'lon')
Inputs may be any that keep to these rules, and one draw needn't show every extreme that they name: `cutoff`: rows 256 to 767 hold 5760/2 (no damping); every other row holds less.
All inputs are finite; a program needn't handle non-finite values.
Results may differ from a plain program's by a relative error of at most 0.000073.
Values sent between devices are 32-bit elements; how exact they have to be, the bound alone decides.
No kernel may reach another device: no remote copies, remote signals or barrier semaphores. Data moves between devices by JAX's collectives and lax.ppermute only.
A program may use at most 64 MiB of HBM per device.

v0:
```python
import math

import jax
import jax.numpy as jnp
from jax import lax
from jax.sharding import PartitionSpec as P

meridional_courant = 0.05
pressure_gain = 4.0
inner_length = 128
highest = lax.Precision.HIGHEST


def with_halo(array, sides, width):
    for axis, dim in sides:
        size, length = (lax.axis_size(axis), array.shape[dim])
        up = [(i, (i + 1) % size) for i in range(size)]
        down = [(j, i) for i, j in up]
        last = lax.slice_in_dim(array, length - width, length, axis=dim)
        first = lax.slice_in_dim(array, 0, width, axis=dim)
        before = lax.ppermute(last, axis, up)
        after = lax.ppermute(first, axis, down)
        array = jnp.concatenate([before, array, after], axis=dim)
    return array


def dft_tables(period):
    positions = jnp.arange(period, dtype=jnp.int32)
    phase_angle = (
        2.0
        * math.pi
        / period
        * (positions[:, None] * positions[None, :] % period).astype(jnp.float32)
    )
    return (jnp.cos(phase_angle), jnp.sin(phase_angle))


def damp_lines(line_values, line_cutoff):
    rows_in = line_values.shape[0]
    line_length = line_values.shape[1]
    outer_length = line_length // inner_length
    cos_outer, sin_outer = dft_tables(outer_length)
    cos_inner, sin_inner = dft_tables(inner_length)
    outer_index = jnp.arange(outer_length, dtype=jnp.int32)
    inner_index = jnp.arange(inner_length, dtype=jnp.int32)
    twist_angle = (
        2.0
        * math.pi
        / line_length
        * (outer_index[:, None] * inner_index[None, :] % line_length).astype(jnp.float32)
    )
    cos_twist = jnp.cos(twist_angle)
    sin_twist = jnp.sin(twist_angle)
    grid_lines = line_values.reshape(rows_in, outer_length, inner_length)
    real_a = jnp.einsum("kn,mnb->mkb", cos_outer, grid_lines, precision=highest)
    imag_a = -jnp.einsum("kn,mnb->mkb", sin_outer, grid_lines, precision=highest)
    real_b = real_a * cos_twist + imag_a * sin_twist
    imag_b = imag_a * cos_twist - real_a * sin_twist
    real_c = jnp.einsum("mkb,bc->mkc", real_b, cos_inner, precision=highest) + jnp.einsum(
        "mkb,bc->mkc", imag_b, sin_inner, precision=highest
    )
    imag_c = jnp.einsum("mkb,bc->mkc", imag_b, cos_inner, precision=highest) - jnp.einsum(
        "mkb,bc->mkc", real_b, sin_inner, precision=highest
    )
    wave_number = outer_index[:, None] + outer_length * inner_index[None, :]
    folded = jnp.minimum(wave_number, line_length - wave_number)
    cut_ratio = line_cutoff[:, None, None] / jnp.maximum(folded, 1).astype(jnp.float32)[None]
    damping = jnp.minimum(1.0, cut_ratio * cut_ratio)
    real_c = real_c * damping
    imag_c = imag_c * damping
    real_g = jnp.einsum("mkc,bc->mkb", real_c, cos_inner, precision=highest) - jnp.einsum(
        "mkc,bc->mkb", imag_c, sin_inner, precision=highest
    )
    imag_g = jnp.einsum("mkc,bc->mkb", imag_c, cos_inner, precision=highest) + jnp.einsum(
        "mkc,bc->mkb", real_c, sin_inner, precision=highest
    )
    real_h = real_g * cos_twist - imag_g * sin_twist
    imag_h = imag_g * cos_twist + real_g * sin_twist
    result = jnp.einsum("kn,mkb->mnb", cos_outer, real_h, precision=highest) - jnp.einsum(
        "kn,mkb->mnb", sin_outer, imag_h, precision=highest
    )
    return (result * (1.0 / line_length)).reshape(rows_in, line_length)


def trim_rims(extended, row_dim):
    band_index = lax.axis_index("lat")
    band_count = lax.axis_size("lat")
    rows_ext = extended.shape[row_dim]
    positions = jnp.arange(rows_ext, dtype=jnp.int32)
    keep_rows = jnp.logical_not(
        (positions == 0) & (band_index == 0)
        | (positions == rows_ext - 1) & (band_index == band_count - 1)
    )
    mask_shape = [1] * extended.ndim
    mask_shape[row_dim] = rows_ext
    return extended * keep_rows.astype(extended.dtype).reshape(mask_shape)


def along_lon(field_ext):
    return (field_ext[..., 1:-1, 2:] - field_ext[..., 1:-1, :-2]) * 0.5


def along_lat(field_ext):
    return (field_ext[..., 2:, 1:-1] - field_ext[..., :-2, 1:-1]) * 0.5


def filter_block(work_block, block_cutoff):
    lon_parts = lax.axis_size("lon")
    components, levels, rows_here, width_here = work_block.shape
    per_part = components * levels * rows_here // lon_parts
    line_values = work_block.reshape(lon_parts, per_part, width_here)
    line_cut = jnp.broadcast_to(
        block_cutoff.astype(jnp.float32)[None, None, :], (components, levels, rows_here)
    ).reshape(lon_parts, per_part, 1)
    circles = lax.all_to_all(line_values, "lon", split_axis=0, concat_axis=2, tiled=True)
    cut_column = lax.all_to_all(line_cut, "lon", split_axis=0, concat_axis=2, tiled=True)
    smoothed = damp_lines(circles[0], cut_column[0, :, 0])
    returned = lax.all_to_all(smoothed[None], "lon", split_axis=2, concat_axis=0, tiled=True)
    return returned.reshape(work_block.shape)


def per_device(model_state, courant, cutoff):
    rows_here = model_state.shape[2]
    band_index = lax.axis_index("lat")
    extended = with_halo(model_state, (("lon", 3), ("lat", 2)), 1)
    extended = trim_rims(extended, 2)
    wind_east = extended[0]
    wind_north = extended[1]
    theta_ext = extended[2]
    thickness = extended[3]
    row_courant = courant[None, :, None]
    east_flux = wind_east * thickness
    north_flux = wind_north * thickness
    heat_content = theta_ext * thickness
    new_thickness = (
        thickness[:, 1:-1, 1:-1]
        - row_courant * along_lon(east_flux)
        - meridional_courant * along_lat(north_flux)
    )
    new_heat = (
        heat_content[:, 1:-1, 1:-1]
        - row_courant * along_lon(east_flux * theta_ext)
        - meridional_courant * along_lat(north_flux * theta_ext)
    )
    new_theta = new_heat / new_thickness
    heat_ext = trim_rims(with_halo(new_heat, (("lon", 2), ("lat", 1)), 1), 1)
    new_east = wind_east[:, 1:-1, 1:-1] - pressure_gain * row_courant * along_lon(heat_ext)
    new_north = wind_north[:, 1:-1, 1:-1] - pressure_gain * meridional_courant * along_lat(heat_ext)
    stacked = jnp.stack([new_east, new_north, new_theta, new_thickness])
    own_cut = lax.dynamic_slice_in_dim(cutoff, band_index * rows_here, rows_here)
    return filter_block(stacked, own_cut)


def solution(mesh):
    placed = (P(None, None, "lat", "lon"), P("lat"), P())
    return jax.shard_map(
        per_device,
        mesh=mesh,
        in_specs=placed,
        out_specs=P(None, None, "lat", "lon"),
        check_vma=False,
    )
```

profile of v0, /device:TPU:88, one launch (start us, length us, event | category | flops | bytes accessed | tf_op | source)
XLA Modules:
  0.0 251.1 jit_solution(1462764432436495926)
XLA Ops:
  0.0 2.3 fusion.164
  4.3 11.7 %collective-permute-start.1 = (f32[4,8,32,1]{3,2,1,0:T(8,128)S(1)}, f32[4,8,32,1]{3,2,1,0:T(8,128)S(1)}, u32[]{:S(2)}, u32[]{:S(2)}) collective-permute-start(f32[4,8,32,1]{3,2,1,0:T(8,128)S(1)} %get-tuple-element.23), channel_id=1, source_target_pairs={{32,0},{64,32},{96,64},{128,96},{160,128},{192,160},{224,192},{256... | collective-permute-start | bytes 12296 | tf_op jit(solution)/shard_map/ppermute | solution.py:22
  16.0 10.9 %collective-permute-done = f32[4,8,32,1]{3,2,1,0:T(8,128)S(1)} collective-permute-done((f32[4,8,32,1]{3,2,1,0:T(8,128)}, f32[4,8,32,1]{3,2,1,0:T(8,128)S(1)}, u32[]{:S(2)}, u32[]{:S(2)}) %collective-permute-start) | collective-permute-done | bytes 4128 | tf_op jit(solution)/shard_map/ppermute | solution.py:21
  28.6 4.7 %collective-permute-start.2 = (f32[4,8,1,362]{3,2,1,0:T(1,128)S(1)}, f32[4,8,1,362]{3,2,1,0:T(1,128)S(1)}, u32[]{:S(2)}, u32[]{:S(2)}) collective-permute-start(f32[4,8,1,362]{3,2,1,0:T(1,128)S(1)} %get-tuple-element.14), channel_id=1, source_target_pairs={{0,1},{1,2},{2,3},{3,4},{4,5},{5,6},{6,7},{7,8},{8,9},{9,10},{10,1... | collective-permute-start | bytes 139016 | tf_op jit(solution)/shard_map/ppermute | solution.py:21
  35.2 5.2 %collective-permute-done.3 = f32[4,8,1,362]{3,2,1,0:T(1,128)S(1)} collective-permute-done((f32[4,8,1,362]{3,2,1,0:T(1,128)S(1)}, f32[4,8,1,362]{3,2,1,0:T(1,128)S(1)}, u32[]{:S(2)}, u32[]{:S(2)}) %collective-permute-start.3) | collective-permute-done | bytes 46368 | tf_op jit(solution)/shard_map/ppermute | solution.py:22
  44.7 9.7 %collective-permute-start.5 = (f32[8,32,1]{2,1,0:T(8,128)S(1)}, f32[8,32,1]{2,1,0:T(8,128)S(1)}, u32[]{:S(2)}, u32[]{:S(2)}) collective-permute-start(f32[8,32,1]{2,1,0:T(8,128)S(1)} %get-tuple-element.29), channel_id=1, source_target_pairs={{32,0},{64,32},{96,64},{128,96},{160,128},{192,160},{224,192},{256... | collective-permute-start | bytes 3080 | tf_op jit(solution)/shard_map/ppermute | solution.py:22
  58.9 3.9 %collective-permute-start.7 = (f32[8,1,362]{2,1,0:T(1,128)S(1)}, f32[8,1,362]{2,1,0:T(1,128)S(1)}, u32[]{:S(2)}, u32[]{:S(2)}) collective-permute-start(f32[8,1,362]{2,1,0:T(1,128)S(1)} %get-tuple-element.25), channel_id=1, source_target_pairs={{1,0},{2,1},{3,2},{4,3},{5,4},{6,5},{7,6},{8,7},{9,8},{10,9},{11,1... | collective-permute-start | bytes 34760 | tf_op jit(solution)/shard_map/ppermute | solution.py:22
  64.3 10.3 %all-to-all-start.1 = ((f32[16,64,1]{1,2,0:T(1,128)}), f32[16,64,1]{1,2,0:T(1,128)S(1)}, u32[]{:S(2)}, u32[]{:S(2)}) async-start(f32[16,64,1]{1,2,0:T(1,128)} %reshape.101), calls=%async_computation.1 | async-start | bytes 16384 | tf_op jit(solution)/shard_map/all_to_all | solution.py:116
  76.8 7.6 %all-to-all-done.1 = f32[16,64,1]{1,2,0:T(1,128)S(1)} async-done(((f32[16,64,1]{1,2,0:T(1,128)}), f32[16,64,1]{1,2,0:T(1,128)S(1)}, u32[]{:S(2)}, u32[]{:S(2)}) %all-to-all-start.1) | async-done | bytes 4128 | tf_op jit(solution)/shard_map/all_to_all | solution.py:116
  84.4 3.9 %all-to-all-start = ((f32[16,64,360]{2,1,0:T(8,128)}), f32[16,64,360]{2,1,0:T(8,128)S(1)}, u32[]{:S(2)}, u32[]{:S(2)}) async-start(f32[16,64,360]{2,1,0:T(8,128)} %bitcast.8), calls=%async_computation | async-start | bytes 3145728 | tf_op jit(solution)/shard_map/all_to_all | solution.py:115
  88.5 42.3 %all-to-all-done = f32[16,64,360]{2,1,0:T(8,128)S(1)} async-done(((f32[16,64,360]{2,1,0:T(8,128)}), f32[16,64,360]{2,1,0:T(8,128)S(1)}, u32[]{:S(2)}, u32[]{:S(2)}) %all-to-all-start) | async-done | bytes 1474592 | tf_op jit(solution)/shard_map/all_to_all | solution.py:115
  140.5 2.2 subtract_multiply_fusion
  142.7 2.5 %fusion.10 = f32[64,45,128]{2,1,0:T(8,128)S(1)} fusion(f32[64,45,128]{2,0,1:T(8,128)S(1)} %subtract_multiply_fusion), kind=kOutput, calls=%fused_computation.17 | convolution fusion | flops 566460416 | bytes 2949120 | tf_op jit(solution)/shard_map/mkc,bc->mkb/dot_general | solution.py:74
  145.2 2.5 %fusion.12 = f32[64,45,128]{2,1,0:T(8,128)S(1)} fusion(f32[64,45,128]{2,0,1:T(8,128)S(1)} %subtract_multiply_fusion), kind=kOutput, calls=%fused_computation.19 | convolution fusion | flops 566460416 | bytes 2949120 | tf_op jit(solution)/shard_map/mkc,bc->mkb/dot_general | solution.py:71
  149.7 2.6 %fusion.21 = f32[64,45,128]{2,1,0:T(8,128)S(1)} fusion(f32[64,45,128]{2,1,0:T(8,128)S(1)} %fusion.10, f32[64,45,128]{2,0,1:T(8,128)S(1)} %add_multiply_fusion), kind=kOutput, calls=%fused_computation.26 | convolution fusion | flops 566829056 | bytes 4423680 | tf_op jit(solution)/shard_map/mkc,bc->mkb/dot_general | solution.py:74
  152.3 3.0 %fusion.18 = f32[64,45,128]{2,1,0:T(8,128)S(1)} fusion(f32[64,45,128]{2,1,0:T(8,128)S(1)} %fusion.12, f32[64,45,128]{2,0,1:T(8,128)S(1)} %add_multiply_fusion), kind=kOutput, calls=%fused_computation.25 | convolution fusion | flops 566829056 | bytes 4423680 | tf_op jit(solution)/shard_map/mkc,bc->mkb/dot_general | solution.py:71
  157.2 3.1 %multiply_bitcast_fusion = f32[64,45,128]{2,1,0:T(8,128)} fusion(f32[64,128,45]{1,2,0:T(8,128)S(1)} %fusion.2, f32[64,45,128]{2,1,0:T(8,128)S(1)} %fusion.21, f32[64,45,128]{2,1,0:T(8,128)S(1)} %fusion.18, f32[45,128]{1,0:T(8,128)S(1)} %get-tuple-element.32, f32[45,128]{1,0:T(8,128)S(1)} %get-tuple-element.33), kind=kOutput, calls=%fused_computation.8 | convolution fusion | flops 200927024 | bytes 5944320 | tf_op jit(solution)/shard_map/kn,mkb->mnb/dot_general | solution.py:79
  160.3 2.4 copy.51
  163.3 26.6 %reduce = f32[5760,64]{1,0:T(8,128)} reduce(f32[5760,1,64]{2,1,0:T(1,128)S(1)} %bitcast.101, f32[]{:T(128)} %broadcast.169), dimensions={1}, to_apply=%bitcast.91.reduce_sub_computation | reduce | bytes 2949124
  189.8 3.2 %reshape.109 = f32[16,1,23040]{2,1,0:T(1,128)S(1)} reshape(f32[5760,64]{1,0:T(8,128)} %reduce) | data formatting | bytes 2949120
  193.1 45.4 %all_to_all.48 = f32[16,1,23040]{2,1,0:T(1,128)S(1)} all-to-all(f32[16,1,23040]{2,1,0:T(1,128)S(1)} %reshape.109), channel_id=1, replica_groups=mesh['lon'=16,'lat'=32] {'lon'}, dimensions={0} | all-to-all | bytes 2949120 | tf_op jit(solution)/shard_map/all_to_all | solution.py:118
  238.5 5.5 %reduce.1 = f32[16,23040]{1,0:T(8,128)} reduce(f32[16,1,23040]{2,1,0:T(1,128)S(1)} %all_to_all.48, f32[]{:T(128)} %broadcast.169), dimensions={1}, to_apply=%all_to_all.42.reduce_sub_computation | reduce | bytes 2949124 | tf_op jit(solution)/shard_map/all_to_all | solution.py:118
  244.0 4.8 %reshape.110 = f32[5760,1,64]{2,1,0:T(1,128)S(1)} reshape(f32[16,23040]{1,0:T(8,128)} %reduce.1) | data formatting | bytes 2949120
  248.9 2.0 copy.40
  (42 shorter events, 32.0 us)
Async XLA Ops:
  0.0 28.2 %copy-start = (f32[4,8,32,360]{3,2,1,0:T(8,128)S(1)}, f32[4,8,32,360]{3,2,1,0:T(8,128)}, u32[]{:S(2)}) copy-start(f32[4,8,32,360]{3,2,1,0:T(8,128)} %param.3) | copy-start | bytes 4423684
  0.0 15.9 %copy-start.1 = (f32[32]{0:T(128)S(1)}, f32[32]{0:T(128)}, u32[]{:S(2)}) copy-start(f32[32]{0:T(128)} %param.4) | copy-start | bytes 388
  2.4 24.6 %collective-permute-start = (f32[4,8,32,1]{3,2,1,0:T(8,128)}, f32[4,8,32,1]{3,2,1,0:T(8,128)S(1)}, u32[]{:S(2)}, u32[]{:S(2)}) collective-permute-start(f32[4,8,32,1]{3,2,1,0:T(8,128)} %get-tuple-element.22), channel_id=1, source_target_pairs={{0,32},{32,64},{64,96},{96,128},{128,160},{160,192},{192,224},{224... | collective-permute-start | bytes 12296 | tf_op jit(solution)/shard_map/ppermute | solution.py:21
  4.3 24.0 %collective-permute-start.1 = (f32[4,8,32,1]{3,2,1,0:T(8,128)S(1)}, f32[4,8,32,1]{3,2,1,0:T(8,128)S(1)}, u32[]{:S(2)}, u32[]{:S(2)}) collective-permute-start(f32[4,8,32,1]{3,2,1,0:T(8,128)S(1)} %get-tuple-element.23), channel_id=1, source_target_pairs={{32,0},{64,32},{96,64},{128,96},{160,128},{192,160},{224,192},{256... | collective-permute-start | bytes 12296 | tf_op jit(solution)/shard_map/ppermute | solution.py:22
  28.6 6.6 %collective-permute-start.2 = (f32[4,8,1,362]{3,2,1,0:T(1,128)S(1)}, f32[4,8,1,362]{3,2,1,0:T(1,128)S(1)}, u32[]{:S(2)}, u32[]{:S(2)}) collective-permute-start(f32[4,8,1,362]{3,2,1,0:T(1,128)S(1)} %get-tuple-element.14), channel_id=1, source_target_pairs={{0,1},{1,2},{2,3},{3,4},{4,5},{5,6},{6,7},{7,8},{8,9},{9,10},{10,1... | collective-permute-start | bytes 139016 | tf_op jit(solution)/shard_map/ppermute | solution.py:21
  33.3 7.2 %collective-permute-start.3 = (f32[4,8,1,362]{3,2,1,0:T(1,128)S(1)}, f32[4,8,1,362]{3,2,1,0:T(1,128)S(1)}, u32[]{:S(2)}, u32[]{:S(2)}) collective-permute-start(f32[4,8,1,362]{3,2,1,0:T(1,128)S(1)} %get-tuple-element.15), channel_id=1, source_target_pairs={{1,0},{2,1},{3,2},{4,3},{5,4},{6,5},{7,6},{8,7},{9,8},{10,9},{11,1... | collective-permute-start | bytes 139016 | tf_op jit(solution)/shard_map/ppermute | solution.py:22
  42.7 12.4 %collective-permute-start.4 = (f32[8,32,1]{2,1,0:T(8,128)S(1)}, f32[8,32,1]{2,1,0:T(8,128)S(1)}, u32[]{:S(2)}, u32[]{:S(2)}) collective-permute-start(f32[8,32,1]{2,1,0:T(8,128)S(1)} %get-tuple-element.28), channel_id=1, source_target_pairs={{0,32},{32,64},{64,96},{96,128},{128,160},{160,192},{192,224},{224... | collective-permute-start | bytes 3080 | tf_op jit(solution)/shard_map/ppermute | solution.py:21
  44.7 12.2 %collective-permute-start.5 = (f32[8,32,1]{2,1,0:T(8,128)S(1)}, f32[8,32,1]{2,1,0:T(8,128)S(1)}, u32[]{:S(2)}, u32[]{:S(2)}) collective-permute-start(f32[8,32,1]{2,1,0:T(8,128)S(1)} %get-tuple-element.29), channel_id=1, source_target_pairs={{32,0},{64,32},{96,64},{128,96},{160,128},{192,160},{224,192},{256... | collective-permute-start | bytes 3080 | tf_op jit(solution)/shard_map/ppermute | solution.py:22
  57.0 17.6 %collective-permute-start.6 = (f32[8,1,362]{2,1,0:T(1,128)S(1)}, f32[8,1,362]{2,1,0:T(1,128)S(1)}, u32[]{:S(2)}, u32[]{:S(2)}) collective-permute-start(f32[8,1,362]{2,1,0:T(1,128)S(1)} %get-tuple-element.24), channel_id=1, source_target_pairs={{0,1},{1,2},{2,3},{3,4},{4,5},{5,6},{6,7},{7,8},{8,9},{9,10},{10,1... | collective-permute-start | bytes 34760 | tf_op jit(solution)/shard_map/ppermute | solution.py:21
  58.9 15.7 %collective-permute-start.7 = (f32[8,1,362]{2,1,0:T(1,128)S(1)}, f32[8,1,362]{2,1,0:T(1,128)S(1)}, u32[]{:S(2)}, u32[]{:S(2)}) collective-permute-start(f32[8,1,362]{2,1,0:T(1,128)S(1)} %get-tuple-element.25), channel_id=1, source_target_pairs={{1,0},{2,1},{3,2},{4,3},{5,4},{6,5},{7,6},{8,7},{9,8},{10,9},{11,1... | collective-permute-start | bytes 34760 | tf_op jit(solution)/shard_map/ppermute | solution.py:22
  64.3 20.2 %all-to-all-start.1 = ((f32[16,64,1]{1,2,0:T(1,128)}), f32[16,64,1]{1,2,0:T(1,128)S(1)}, u32[]{:S(2)}, u32[]{:S(2)}) async-start(f32[16,64,1]{1,2,0:T(1,128)} %reshape.101), calls=%async_computation.1 | async-start | bytes 16384 | tf_op jit(solution)/shard_map/all_to_all | solution.py:116
  84.4 46.4 %all-to-all-start = ((f32[16,64,360]{2,1,0:T(8,128)}), f32[16,64,360]{2,1,0:T(8,128)S(1)}, u32[]{:S(2)}, u32[]{:S(2)}) async-start(f32[16,64,360]{2,1,0:T(8,128)} %bitcast.8), calls=%async_computation | async-start | bytes 3145728 | tf_op jit(solution)/shard_map/all_to_all | solution.py:115
where the time goes:
time: 256 us; the launch traced here: 251 us
  waiting for transfers between devices  70 us (27%)
  starting transfers between devices  51.8 us (20%)
  blocking collectives  45.4 us (18%)
  other arithmetic  37.7 us (15%)
  matrix products  27 us (11%)
  local copies, waits for them, and re-layouts  18.6 us (7%)
    all_to_all x1, blocking collectives, filter_block(): lax.all_to_all(smoothed[None], 'lon', split_axis=2, concat_axis=0, tiled=...  45.4 us
    all_to_all x1, waiting for transfers between devices, filter_block(): lax.all_to_all(line_values, 'lon', split_axis=0, concat_axis=2, tiled=True)  42.3 us
    ppermute x4, starting transfers between devices, with_halo(): after = lax.ppermute(first, axis, down)  27.2 us
    unnamed x1, other arithmetic  26.6 us
    ppermute x4, waiting for transfers between devices, with_halo(): before = lax.ppermute(last, axis, up)  11.7 us
    ppermute x4, starting transfers between devices, with_halo(): before = lax.ppermute(last, axis, up)  10.4 us
    all_to_all x1, starting transfers between devices, filter_block(): lax.all_to_all(line_cut, 'lon', split_axis=0, concat_axis=2, tiled=True)  10.3 us
    unnamed x7, local copies, waits for them, and re-layouts  8.59 us
  transfers between devices with their start and end apart: 10, of which 7 were waited for; matrix products, arithmetic and copies ran while one was open for 2% of the time, Pallas kernels for 0%

commit v1 on v0

v1 whole, which is shorter than its diff:
```python
import math

import jax
import jax.numpy as jnp
import numpy as np
from jax import lax
from jax.experimental import pallas as pl
from jax.experimental.pallas import tpu as pltpu
from jax.sharding import PartitionSpec as P

slabs = 16
width = 360
circle = slabs * width
lanes = 384
fields = 4
half_rows = 16
lines = fields * half_rows
halo_lines = 8
freqs = slabs // 2 + 1

cross = 0.05 * 0.5
push_north = 4.0 * 0.05 * 0.5
push_east = 4.0 * 0.5


def width_tables():
    r = np.arange(width)
    angle = 2.0 * np.pi * ((r[:, None] * r[None, :]) % width) / width
    cos, sin = np.cos(angle), np.sin(angle)
    table = np.zeros((2 * lanes, 2 * lanes), np.float64)
    table[:width, :width] = cos
    table[:width, lanes : lanes + width] = -sin
    table[lanes : lanes + width, :width] = sin
    table[lanes : lanes + width, lanes : lanes + width] = cos
    high = table.astype(jnp.bfloat16)
    low = (table - high.astype(np.float64)).astype(jnp.bfloat16)
    return high, low


def line_tables():
    r = np.arange(width)
    twist = np.zeros((2, slabs, lanes), np.float32)
    inverse = np.zeros((freqs, 1, 2 * lanes), np.float32)
    for k in range(freqs):
        angle = 2.0 * np.pi * (k * r) / circle
        twist[0, k, :width] = np.cos(angle)
        twist[1, k, :width] = np.sin(angle)
        wave = k + slabs * r
        folded = np.maximum(np.minimum(wave, circle - wave), 1)
        inverse[k, 0, :width] = 1.0 / folded
        inverse[k, 0, lanes : lanes + width] = 1.0 / folded
    return twist, inverse


def real_forward(x):
    n = len(x)
    if n == 1:
        return [(x[0], None)]
    if n == 2:
        return [(x[0] + x[1], None), (x[0] - x[1], None)]
    even, odd = real_forward(x[0::2]), real_forward(x[1::2])
    out = [None] * (n // 2 + 1)
    out[0] = (even[0][0] + odd[0][0], None)
    out[n // 2] = (even[0][0] - odd[0][0], None)
    out[n // 4] = (even[n // 4][0], -odd[n // 4][0])
    for k in range(1, n // 4):
        c, s = math.cos(2 * math.pi * k / n), math.sin(2 * math.pi * k / n)
        (er, ei), (qr, qi) = even[k], odd[k]
        if 8 * k == n:
            tr, ti = (qr + qi) * c, (qi - qr) * c
        else:
            tr, ti = qr * c + qi * s, qi * c - qr * s
        out[k] = (er + tr, ei + ti)
        out[n // 2 - k] = (er - tr, ti - ei)
    return out


def real_inverse(bins):
    n = 2 * (len(bins) - 1)
    if n == 2:
        return [bins[0][0] + bins[1][0], bins[0][0] - bins[1][0]]
    even, odd = [None] * (n // 4 + 1), [None] * (n // 4 + 1)
    even[0] = (bins[0][0] + bins[n // 2][0], None)
    odd[0] = (bins[0][0] - bins[n // 2][0], None)
    mid = bins[n // 4]
    even[n // 4] = (mid[0] + mid[0], None)
    odd[n // 4] = (-(mid[1] + mid[1]), None)
    for k in range(1, n // 4):
        c, s = math.cos(2 * math.pi * k / n), math.sin(2 * math.pi * k / n)
        (ar, ai), (br, bi) = bins[k], bins[n // 2 - k]
        even[k] = (ar + br, ai - bi)
        dr, di = ar - br, ai + bi
        if 8 * k == n:
            odd[k] = ((dr - di) * c, (di + dr) * c)
        else:
            odd[k] = (dr * c - di * s, di * c + dr * s)
    evens, odds = real_inverse(even), real_inverse(odd)
    out = [None] * n
    out[0::2], out[1::2] = evens, odds
    return out


def circle_kernel(
    raw, courant, cutoff, rim, twist, inverse, high, low, out, flux_a, flux_b, heat, heat_rim, work, part_high, part_low, spectrum
):
    lane = lax.broadcasted_iota(jnp.int32, (half_rows, lanes), 1)
    row = lax.broadcasted_iota(jnp.int32, (half_rows, lanes), 0)
    valid = lane < width

    def after(value, follower):
        return jnp.where(lane[: value.shape[0]] == width - 1, follower, pltpu.roll(value, lanes - 1, 1))

    def before(value, leader):
        return jnp.where(lane[: value.shape[0]] == 0, leader, pltpu.roll(value, 1, 1))

    def sides(s):
        return lax.rem(s + 1, slabs), lax.rem(s + slabs - 1, slabs)

    def north_minus_south(value, top, bottom):
        ahead = jnp.where(row == half_rows - 1, bottom, pltpu.roll(value, half_rows - 1, 0))
        behind = jnp.where(row == 0, top, pltpu.roll(value, 1, 0))
        return ahead - behind

    def east_minus_west(ref, s):
        ahead, behind = sides(s)
        value = ref[s]
        return after(value, ref[ahead, :, 0:1]) - before(value, ref[behind, :, width - 1 : width])

    def products(s, carry):
        flux = raw[s, 0:16, :] * raw[s, 48:64, :]
        flux_a[s] = flux
        flux_b[s] = flux * raw[s, 32:48, :]
        return carry

    lax.fori_loop(0, slabs, products, 0)

    def advance(s, carry):
        theta, thick = raw[s, 32:48, :], raw[s, 48:64, :]
        north = raw[s, 16:32, :] * thick
        north_heat = north * theta
        pace = courant[...] * 0.5
        new_thick = (
            thick
            - pace * east_minus_west(flux_a, s)
            - cross * north_minus_south(north, raw[s, 70:71, :], raw[s, 71:72, :])
        )
        new_heat = (
            theta * thick
            - pace * east_minus_west(flux_b, s)
            - cross * north_minus_south(north_heat, raw[s, 68:69, :], raw[s, 69:70, :])
        )
        heat[s] = new_heat
        work[s, 48:64, :] = jnp.where(valid, new_thick, 0.0)
        work[s, 32:48, :] = jnp.where(valid, new_heat / new_thick, 0.0)
        ahead, behind = sides(s)
        slope = after(raw[s, 66:68, :], raw[ahead, 66:68, 0:1]) - before(
            raw[s, 66:68, :], raw[behind, 66:68, width - 1 : width]
        )
        inner = jnp.concatenate([-north_heat[0:1], north_heat[half_rows - 1 : half_rows]], axis=0)
        heat_rim[s] = (raw[s, 64:66, :] - 0.5 * slope + cross * inner) * rim[...]
        return carry

    lax.fori_loop(0, slabs, advance, 0)

    def push(s, carry):
        new_east = raw[s, 0:16, :] - (push_east * courant[...]) * east_minus_west(heat, s)
        new_north = raw[s, 16:32, :] - push_north * north_minus_south(heat[s], heat_rim[s, 0:1, :], heat_rim[s, 1:2, :])
        work[s, 0:16, :] = jnp.where(valid, new_east, 0.0)
        work[s, 16:32, :] = jnp.where(valid, new_north, 0.0)
        return carry

    lax.fori_loop(0, slabs, push, 0)

    def split_into(rows, columns, value):
        upper = value.astype(jnp.bfloat16)
        part_high[rows, columns] = upper
        part_low[rows, columns] = (value - upper.astype(jnp.float32)).astype(jnp.bfloat16)

    def across(f, carry):
        for tile in range(lanes // 128):
            here = slice(tile * 128, tile * 128 + 128)
            there = slice(lanes + tile * 128, lanes + tile * 128 + 128)
            bins = real_forward([work[s, pl.ds(f * half_rows, half_rows), here] for s in range(slabs)])
            for k, (re, im) in enumerate(bins):
                rows = pl.ds(k * lines + f * half_rows, half_rows)
                if k == 0:
                    split_into(rows, here, re)
                    split_into(rows, there, jnp.zeros_like(re))
                    continue
                cos, sin = twist[0, k : k + 1, here], twist[1, k : k + 1, here]
                if im is None:
                    split_into(rows, here, re * cos)
                    split_into(rows, there, -(re * sin))
                else:
                    split_into(rows, here, re * cos + im * sin)
                    split_into(rows, there, im * cos - re * sin)
        return carry

    lax.fori_loop(0, fields, across, 0)

    def along(n, carry):
        columns = pl.ds(pl.multiple_of(n * 256, 256), 256)
        table = high[:, columns]
        total = jnp.dot(part_high[...], table, preferred_element_type=jnp.float32)
        total += jnp.dot(part_low[...], table, preferred_element_type=jnp.float32)
        total += jnp.dot(part_high[...], low[:, columns], preferred_element_type=jnp.float32)
        spectrum[:, columns] = total
        return carry

    lax.fori_loop(0, 2 * lanes // 256, along, 0)

    def damp(k, carry):
        for tile in range(2 * lanes // 128):
            here = slice(tile * 128, tile * 128 + 128)
            target = (tile + lanes // 128) % (2 * lanes // 128)
            there = slice(target * 128, target * 128 + 128)
            ratio = cutoff[...] * inverse[k, :, here]
            factor = jnp.minimum(1.0, ratio * ratio) * (1.0 / circle)
            for f in range(fields):
                rows = pl.ds(pl.multiple_of(k * lines + f * half_rows, half_rows), half_rows)
                split_into(rows, there, spectrum[rows, here] * factor)
        return carry

    lax.fori_loop(0, freqs, damp, 0)
    lax.fori_loop(0, 2 * lanes // 256, along, 0)

    def back(f, carry):
        for tile in range(lanes // 128):
            here = slice(tile * 128, tile * 128 + 128)
            there = slice(lanes + tile * 128, lanes + tile * 128 + 128)
            bins = []
            for k in range(freqs):
                rows = pl.ds(pl.multiple_of(k * lines + f * half_rows, half_rows), half_rows)
                re = spectrum[rows, there]
                if k == 0:
                    bins.append((re, None))
                    continue
                im = spectrum[rows, here]
                cos, sin = twist[0, k : k + 1, here], twist[1, k : k + 1, here]
                turned = re * cos - im * sin
                bins.append((turned, None if k == freqs - 1 else im * cos + re * sin))
            for s, value in enumerate(real_inverse(bins)):
                out[s, pl.ds(f * half_rows, half_rows), here] = value
        return carry

    lax.fori_loop(0, fields, back, 0)


def filter_circles(raw, courant, cutoff, rim):
    twist, inverse = line_tables()
    high, low = width_tables()
    scratch = [
        pltpu.VMEM((slabs, half_rows, lanes), jnp.float32),
        pltpu.VMEM((slabs, half_rows, lanes), jnp.float32),
        pltpu.VMEM((slabs, half_rows, lanes), jnp.float32),
        pltpu.VMEM((slabs, 2, lanes), jnp.float32),
        pltpu.VMEM((slabs, lines, lanes), jnp.float32),
        pltpu.VMEM((freqs * lines, 2 * lanes), jnp.bfloat16),
        pltpu.VMEM((freqs * lines, 2 * lanes), jnp.bfloat16),
        pltpu.VMEM((freqs * lines, 2 * lanes), jnp.float32),
    ]
    return pl.pallas_call(
        circle_kernel,
        out_shape=jax.ShapeDtypeStruct((slabs, lines, lanes), jnp.float32),
        in_specs=[pl.BlockSpec(memory_space=pltpu.VMEM)] * 8,
        out_specs=pl.BlockSpec(memory_space=pltpu.VMEM),
        scratch_shapes=scratch,
        compiler_params=pltpu.CompilerParams(vmem_limit_bytes=40 << 20),
        name="circles",
    )(raw, courant, cutoff, rim, jnp.asarray(twist), jnp.asarray(inverse), jnp.asarray(high), jnp.asarray(low))


def rim_terms(block, courant, row, inner):
    east, north, theta, thick = (block[i, :, row] for i in range(4))
    heat = theta * thick
    north_flux = north * thick
    sign = 1.0 if inner < row else -1.0
    outer = block[1, :, inner] * block[3, :, inner] * block[2, :, inner]
    return jnp.stack([heat + sign * cross * outer, courant[row] * (east * heat), north_flux * theta, north_flux])


def on_circles(block, courant, cutoff, top, bottom):
    levels, rows_here = block.shape[1:3]
    count = lax.axis_size("lat")
    band = lax.axis_index("lat")
    half = lax.axis_index("lon") % 2
    main = block.reshape(fields, levels, 2, half_rows, width).transpose(1, 2, 0, 3, 4).reshape(slabs, lines, width)
    tops = jnp.stack([top, rim_terms(block, courant, half_rows - 1, half_rows - 2)], axis=2)
    bottoms = jnp.stack([rim_terms(block, courant, half_rows, half_rows + 1), bottom], axis=2)
    rims = jnp.stack([tops, bottoms], axis=3).transpose(1, 2, 0, 3, 4).reshape(slabs, halo_lines, width)
    sent = jnp.pad(jnp.concatenate([main, rims], axis=1), ((0, 0), (0, 0), (0, lanes - width)))
    raw = lax.all_to_all(sent, "lon", 0, 0, tiled=True)
    own_courant = lax.dynamic_slice_in_dim(courant, half * half_rows, half_rows)
    own_cutoff = lax.dynamic_slice_in_dim(cutoff, band * rows_here + half * half_rows, half_rows).astype(jnp.float32)
    inside = jnp.stack([jnp.logical_or(band > 0, half > 0), jnp.logical_or(band < count - 1, half < 1)])
    smooth = filter_circles(
        raw,
        jnp.broadcast_to(own_courant[:, None], (half_rows, lanes)),
        jnp.broadcast_to(own_cutoff[:, None], (half_rows, 128)),
        jnp.broadcast_to(inside.astype(jnp.float32)[:, None], (2, lanes)),
    )
    returned = lax.all_to_all(smooth, "lon", 0, 0, tiled=True)
    returned = returned.reshape(levels, 2, fields, half_rows, lanes).transpose(2, 0, 1, 3, 4)
    return returned.reshape(fields, levels, rows_here, lanes)[..., :width]


def east_minus_west(value):
    return value[..., 2:] - value[..., :-2]


def north_minus_south(value, top, bottom):
    extended = jnp.concatenate([top[:, None], value, bottom[:, None]], axis=1)
    return extended[:, 2:] - extended[:, :-2]


def on_blocks(block, courant, cutoff, top, bottom):
    del cutoff
    levels, rows_here, width_here = block.shape[1:]
    count = lax.axis_size("lon")
    wind_east, wind_north, theta, thick = block[0], block[1], block[2], block[3]
    pace = courant[None, :, None] * 0.5
    east = wind_east * thick
    east_heat = east * theta
    north = wind_north * thick
    north_heat = north * theta
    heat = theta * thick - cross * north_minus_south(north_heat, top[2], bottom[2])
    slow = thick - cross * north_minus_south(north, top[3], bottom[3])

    def edge(at, inner, sign):
        pieces = [heat[..., at] + sign * pace[..., 0] * east_heat[..., inner], east_heat[..., at], east[..., at]]
        flat = [p.reshape(-1) for p in pieces] + [top[1][:, at], bottom[1][:, at]]
        return jnp.concatenate(flat)

    onward = [(i, (i + 1) % count) for i in range(count)]
    backward = [(j, i) for i, j in onward]
    west = lax.ppermute(edge(width_here - 1, width_here - 2, 1.0), "lon", onward)
    east_side = lax.ppermute(edge(0, 1, -1.0), "lon", backward)
    plane = levels * rows_here

    def opened(flat):
        three = flat[: 3 * plane].reshape(3, levels, rows_here, 1)
        two = flat[3 * plane :].reshape(2, levels, 1)
        return three, two

    (west_heat, west_east_heat, west_east), west_rims = opened(west)
    (east_heat_side, east_east_heat, east_east), east_rims = opened(east_side)
    wide = jnp.concatenate([west_east, east, east_east], axis=-1)
    wide_heat = jnp.concatenate([west_east_heat, east_heat, east_east_heat], axis=-1)
    new_thick = slow - pace * east_minus_west(wide)
    new_heat = heat - pace * east_minus_west(wide_heat)
    beyond_west = west_heat - pace * east_heat[..., :1]
    beyond_east = east_heat_side + pace * east_heat[..., -1:]
    top_flux = jnp.concatenate([west_rims[0], top[1], east_rims[0]], axis=-1)
    bottom_flux = jnp.concatenate([west_rims[1], bottom[1], east_rims[1]], axis=-1)
    top_heat = top[0] - 0.5 * east_minus_west(top_flux) - cross * north_heat[:, 0]
    bottom_heat = bottom[0] - 0.5 * east_minus_west(bottom_flux) + cross * north_heat[:, -1]
    new_east = wind_east - 4.0 * pace * east_minus_west(jnp.concatenate([beyond_west, new_heat, beyond_east], axis=-1))
    new_north = wind_north - push_north * north_minus_south(new_heat, top_heat, bottom_heat)
    return jnp.stack([new_east, new_north, new_heat / new_thick, new_thick])


def per_device(model_state, courant, cutoff):
    rows_here = model_state.shape[2]
    count = lax.axis_size("lat")
    band = lax.axis_index("lat")
    up = [(i, i + 1) for i in range(count - 1)]
    down = [(i + 1, i) for i in range(count - 1)]
    top = lax.ppermute(rim_terms(model_state, courant, rows_here - 1, rows_here - 2), "lat", up)
    bottom = lax.ppermute(rim_terms(model_state, courant, 0, 1), "lat", down)
    polar = jnp.logical_or(4 * band < count, 4 * band >= 3 * count)
    return lax.cond(polar, on_circles, on_blocks, model_state, courant, cutoff, top, bottom)


def solution(mesh):
    placed = (P(None, None, "lat", "lon"), P("lat"), P())
    return jax.shard_map(
        per_device,
        mesh=mesh,
        in_specs=placed,
        out_specs=P(None, None, "lat", "lon"),
        check_vma=False,
    )
```

time: 256 us -> 108 us (0.42)
  the two profiles are of different devices: /device:TPU:88 before, /device:TPU:192 now
where the time goes in v1:
time: 108 us; the launch traced here: 107 us
  waiting for transfers between devices  33.4 us (31%)
  blocking collectives  29.5 us (27%)
  starting transfers between devices  17.6 us (16%)
  Pallas kernels  10.5 us (10%)
  local copies, waits for them, and re-layouts  8.51 us (8%)
  other arithmetic  7.82 us (7%)
    all_to_all x1, blocking collectives, on_circles(): returned = lax.all_to_all(smooth, 'lon', 0, 0, tiled=True)  29.5 us
    all_to_all x1, waiting for transfers between devices, on_circles(): raw = lax.all_to_all(sent, 'lon', 0, 0, tiled=True)  27.2 us
    all_to_all x1, starting transfers between devices, on_circles(): raw = lax.all_to_all(sent, 'lon', 0, 0, tiled=True)  11.2 us
    pallas_call x1, Pallas kernels, filter_circles(): pl.pallas_call(circle_kernel, out_shape=jax.ShapeDtypeStruct((slabs, line...  10.5 us
    ppermute x1, waiting for transfers between devices, per_device(): lax.ppermute(rim_terms(model_state, courant, rows_here - 1, rows_here - 2...  6.14 us
    ppermute x1, starting transfers between devices, per_device(): bottom = lax.ppermute(rim_terms(model_state, courant, 0, 1), 'lat', down)  4.47 us
    add x2, other arithmetic, rim_terms(): heat + sign * cross * outer  2.85 us
    slice x2, local copies, waits for them, and re-layouts, rim_terms(): courant[row] * (east * heat)  2.68 us
  transfers between devices with their start and end apart: 3, of which 2 were waited for; matrix products, arithmetic and copies ran while one was open for 1% of the time, Pallas kernels for 0%

profile of v1, /device:TPU:192, one launch (start us, length us, event | category | flops | bytes accessed | tf_op | source)
XLA Modules:
  0.0 107.5 jit_solution(3184632345287505872)
XLA Ops:
  0.0 1.3 %fusion.68 = (f32[1]{0:T(128)}, f32[1]{0:T(128)}) fusion(f32[32]{0:T(128)} %param.10), kind=kLoop, calls=%fused_computation.146 | loop fusion | bytes 16 | tf_op jit(solution)/shard_map/slice | solution.py:279
  1.3 1.7 %bitcast_multiply_fusion.11 = (f32[1,8,360]{2,0,1:T(1,128)S(1)}, f32[1,8,360]{2,0,1:T(1,128)S(1)}, f32[1,8,360]{2,0,1:T(1,128)S(1)}) fusion(f32[4,8,32,360]{3,2,1,0:T(8,128)} %param.9, f32[]{:T(128)} %bitcast.56), kind=kLoop, calls=%fused_computation.139 | loop fusion | flops 14400 | bytes 80644 | tf_op jit(solution)/shard_map/mul | solution.py:279
  3.1 2.1 %fusion.51 = (f32[1,8,360]{2,0,1:T(1,128)S(1)}, f32[1,8,360]{2,0,1:T(1,128)S(1)}, f32[1,8,360]{2,0,1:T(1,128)S(1)}, f32[1,8,360]{2,0,1:T(1,128)S(1)}, f32[1,8,360]{2,0,1:T(1,128)S(1)}) fusion(f32[4,8,32,360]{3,2,1,0:T(8,128)} %param.9, f32[]{:T(128)} %bitcast.62), kind=kLoop, calls=%fused_computation.126 | loop fusion | flops 40320 | bytes 195844 | tf_op jit(solution)/shard_map/add | solution.py:279
  5.2 4.5 %collective-permute-start.2 = (f32[4,8,360]{2,0,1:T(4,128)S(1)}, f32[4,8,360]{2,0,1:T(4,128)S(1)}, u32[]{:S(2)}, u32[]{:S(2)}) collective-permute-start(f32[4,8,360]{2,0,1:T(4,128)S(1)} %pad_maximum_fusion.17), channel_id=1, source_target_pairs={{1,0},{2,1},{3,2},{4,3},{5,4},{6,5},{7,6},{8,7},{9,8},{10,9},{11,1... | collective-permute-start | bytes 138248 | tf_op jit(solution)/shard_map/ppermute | solution.py:369
  9.8 1.9 %collective-permute-start.3 = (f32[4,8,360]{2,0,1:T(4,128)S(1)}, f32[4,8,360]{2,0,1:T(4,128)S(1)}, u32[]{:S(2)}, u32[]{:S(2)}) collective-permute-start(f32[4,8,360]{2,0,1:T(4,128)S(1)} %pad_maximum_fusion.18), channel_id=1, source_target_pairs={{0,1},{1,2},{2,3},{3,4},{4,5},{5,6},{6,7},{7,8},{8,9},{9,10},{10,1... | collective-permute-start | bytes 138248 | tf_op jit(solution)/shard_map/ppermute | solution.py:368
  11.7 6.1 %collective-permute-done.3 = f32[4,8,360]{2,0,1:T(4,128)S(1)} collective-permute-done((f32[4,8,360]{2,0,1:T(4,128)S(1)}, f32[4,8,360]{2,0,1:T(4,128)S(1)}, u32[]{:S(2)}, u32[]{:S(2)}) %collective-permute-start.3) | collective-permute-done | bytes 46112 | tf_op jit(solution)/shard_map/ppermute | solution.py:368
  17.9 89.6 %conditional.1 = (f32[4,8,32,360]{3,2,1,0:T(8,128)}) conditional(s32[]{:T(128)} %convert_element_type.15, (f32[4,8,32,360]{3,2,1,0:T(8,128)}, f32[32]{0:T(128)}, f32[4,8,360]{2,0,1:T(4,128)S(1)}, f32[4,8,360]{2,0,1:T(4,128)S(1)}) %tuple.11, (f32[4,8,32,360]{3,2,1,0:T(8,128)}, f32[4,8,360]{2,0,1:T(4,128)S(1)}, f32[32]{0:T(128)}, ...), branch_computations={%region_0.0_spmd, %region_1.2_spmd} | conditional | flops 4466144 | bytes 33403902 | solution.py:371
  17.9 1.4 %fusion.62 = (f32[1]{0:T(128)}, f32[1]{0:T(128)}) fusion(f32[32]{0:T(128)} %get-tuple-element.40), kind=kLoop, calls=%fused_computation.140 | loop fusion | bytes 16 | tf_op jit(solution)/shard_map/cond/branch_1_fun/slice | solution.py:279
  19.3 2.5 %copy.386 = f32[4,8,32,360]{3,0,2,1:T(4,128)S(1)} copy(f32[4,8,32,360]{3,2,1,0:T(8,128)} %get-tuple-element.185) | data formatting | bytes 2949120 | tf_op jit(solution)/shard_map
  21.7 0.7 fusion.10
  22.4 0.8 bitcast_add_fusion.1
  23.1 0.1 maximum_bitcast_fusion.3
  23.4 0.2 copy.367
  23.6 0.1 reshape.534
  23.7 0.1 copy.366
  23.9 1.4 %select_maximum_fusion = f32[16,72,384]{2,1,0:T(8,128)} fusion(f32[16,8,360]{2,1,0:T(8,128)S(1)} %reshape.534, f32[16,64,360]{2,1,0:T(8,128)S(1)} %bitcast.294), kind=kLoop, calls=%fused_computation | loop fusion | flops 1769472 | bytes 3428352 | tf_op jit(solution)/shard_map/cond/branch_1_fun/concatenate | solution.py:291
  25.3 11.2 %all-to-all-start = ((f32[16,72,384]{2,1,0:T(8,128)}), f32[16,72,384]{2,1,0:T(8,128)S(1)}, u32[]{:S(2)}, u32[]{:S(2)}) async-start(f32[16,72,384]{2,1,0:T(8,128)} %select_maximum_fusion), calls=%async_computation | async-start | bytes 3538944 | tf_op jit(solution)/shard_map/cond/branch_1_fun/all_to_all | solution.py:292
  36.5 0.1 dynamic_slice.4
  36.7 0.8 dynamic-slice_convert_fusion
  37.4 27.2 %all-to-all-done.raw = f32[16,72,384]{2,1,0:T(8,128)S(1)} async-done(((f32[16,72,384]{2,1,0:T(8,128)}), f32[16,72,384]{2,1,0:T(8,128)S(1)}, u32[]{:S(2)}, u32[]{:S(2)}) %all-to-all-start) | async-done | bytes 1769504 | tf_op jit(solution)/shard_map/cond/branch_1_fun/all_to_all | solution.py:292
  64.9 1.3 %copy-done.1 = bf16[768,768]{1,0:T(8,128)(2,1)S(1)} copy-done((bf16[768,768]{1,0:T(8,128)(2,1)S(1)}, bf16[768,768]{1,0:T(8,128)(2,1)}, u32[]{:S(2)}) %copy-start.1) | copy-done | bytes 1179672 | tf_op jit(solution)/shard_map/cond
  66.1 10.5 %circles.1 = f32[16,64,384]{2,1,0:T(8,128)S(1)} custom-call(f32[16,72,384]{2,1,0:T(8,128)S(1)} %all-to-all-done.raw, f32[16,384]{1,0:T(8,128)S(1)} %broadcast_in_dim.10.courant, f32[16,128]{1,0:T(8,128)S(1)} %broadcast_in_dim.11.cutoff, f32[2,384]{1,0:T(2,128)S(1)} %broadcast_in_dim.12.rim, f32[2,16,384]{2,1,0:T(8,128)S(1)} %copy-done.2, ...), custom_call_target="tpu_custom_call" | custom-call | tf_op jit(solution)/shard_map/cond/branch_1_fun/circles/pallas_call | solution.py:262
  76.6 29.5 %all_to_all.8 = f32[16,64,384]{2,1,0:T(8,128)S(1)} all-to-all(f32[16,64,384]{2,1,0:T(8,128)S(1)} %circles.1), channel_id=1, replica_groups=mesh['lon'=16,'lat'=32] {'lon'}, dimensions={0} | all-to-all | bytes 3145728 | tf_op jit(solution)/shard_map/cond/branch_1_fun/all_to_all | solution.py:302
  106.1 1.4 %copy.368 = f32[8,2,4,16,384]{4,3,1,0,2:T(8,128)} copy(f32[8,2,4,16,384]{4,3,2,1,0:T(8,128)S(1)} %bitcast.295) | data formatting | bytes 3145728 | tf_op jit(solution)/shard_map/cond/branch_1_fun/reshape | solution.py:303
  (27 shorter events, 0.5 us)
Async XLA Ops:
  5.2 6.5 %collective-permute-start.2 = (f32[4,8,360]{2,0,1:T(4,128)S(1)}, f32[4,8,360]{2,0,1:T(4,128)S(1)}, u32[]{:S(2)}, u32[]{:S(2)}) collective-permute-start(f32[4,8,360]{2,0,1:T(4,128)S(1)} %pad_maximum_fusion.17), channel_id=1, source_target_pairs={{1,0},{2,1},{3,2},{4,3},{5,4},{6,5},{7,6},{8,7},{9,8},{10,9},{11,1... | collective-permute-start | bytes 138248 | tf_op jit(solution)/shard_map/ppermute | solution.py:369
  9.8 8.1 %collective-permute-start.3 = (f32[4,8,360]{2,0,1:T(4,128)S(1)}, f32[4,8,360]{2,0,1:T(4,128)S(1)}, u32[]{:S(2)}, u32[]{:S(2)}) collective-permute-start(f32[4,8,360]{2,0,1:T(4,128)S(1)} %pad_maximum_fusion.18), channel_id=1, source_target_pairs={{0,1},{1,2},{2,3},{3,4},{4,5},{5,6},{6,7},{7,8},{8,9},{9,10},{10,1... | collective-permute-start | bytes 138248 | tf_op jit(solution)/shard_map/ppermute | solution.py:368
  17.9 1.4 %copy-start.7 = (f32[4,8,360]{2,0,1:T(4,128)}, f32[4,8,360]{2,0,1:T(4,128)S(1)}, u32[]{:S(2)}) copy-start(f32[4,8,360]{2,0,1:T(4,128)S(1)} %get-tuple-element.41) | copy-start | bytes 138244 | tf_op jit(solution)/shard_map/cond
  17.9 1.4 %copy-start.9 = (f32[4,8,360]{2,0,1:T(4,128)}, f32[4,8,360]{2,0,1:T(4,128)S(1)}, u32[]{:S(2)}) copy-start(f32[4,8,360]{2,0,1:T(4,128)S(1)} %get-tuple-element.39) | copy-start | bytes 138244 | tf_op jit(solution)/shard_map/cond
  19.2 4.0 %copy-start.10 = (f32[4,8,360]{2,0,1:T(4,128)S(1)}, f32[4,8,360]{2,0,1:T(4,128)}, u32[]{:S(2)}) copy-start(f32[4,8,360]{2,0,1:T(4,128)} %copy-done.9) | copy-start | bytes 138244 | tf_op jit(solution)/shard_map/cond
  19.2 4.1 %copy-start.8 = (f32[4,8,360]{2,0,1:T(4,128)S(1)}, f32[4,8,360]{2,0,1:T(4,128)}, u32[]{:S(2)}) copy-start(f32[4,8,360]{2,0,1:T(4,128)} %copy-done.7) | copy-start | bytes 138244 | tf_op jit(solution)/shard_map/cond
  25.3 11.2 %copy-start.16 = (f32[32]{0:T(128)S(1)}, f32[32]{0:T(128)}, u32[]{:S(2)}) copy-start(f32[32]{0:T(128)} %get-tuple-element.40) | copy-start | bytes 388 | tf_op jit(solution)/shard_map/cond
  25.3 39.6 %copy-start = (bf16[768,768]{1,0:T(8,128)(2,1)S(1)}, bf16[768,768]{1,0:T(8,128)(2,1)}, u32[]{:S(2)}) copy-start(bf16[768,768]{1,0:T(8,128)(2,1)} %constant.77.clone.1.low) | copy-start | bytes 3538948 | tf_op jit(solution)/shard_map/cond
  25.3 39.6 %copy-start.2 = (f32[2,16,384]{2,1,0:T(8,128)S(1)}, f32[2,16,384]{2,1,0:T(8,128)}, u32[]{:S(2)}) copy-start(f32[2,16,384]{2,1,0:T(8,128)} %constant.74.clone.1.twist) | copy-start | bytes 147460 | tf_op jit(solution)/shard_map/cond
  25.3 39.6 %copy-start.3 = (f32[9,1,768]{2,1,0:T(1,128)S(1)}, f32[9,1,768]{2,1,0:T(1,128)}, u32[]{:S(2)}) copy-start(f32[9,1,768]{2,1,0:T(1,128)} %constant.75.clone.1.inverse) | copy-start | bytes 82948 | tf_op jit(solution)/shard_map/cond
  25.3 39.4 %all-to-all-start = ((f32[16,72,384]{2,1,0:T(8,128)}), f32[16,72,384]{2,1,0:T(8,128)S(1)}, u32[]{:S(2)}, u32[]{:S(2)}) async-start(f32[16,72,384]{2,1,0:T(8,128)} %select_maximum_fusion), calls=%async_computation | async-start | bytes 3538944 | tf_op jit(solution)/shard_map/cond/branch_1_fun/all_to_all | solution.py:292
  64.9 1.3 %copy-start.1 = (bf16[768,768]{1,0:T(8,128)(2,1)S(1)}, bf16[768,768]{1,0:T(8,128)(2,1)}, u32[]{:S(2)}) copy-start(bf16[768,768]{1,0:T(8,128)(2,1)} %constant.76.clone.1.high) | copy-start | bytes 3538948 | tf_op jit(solution)/shard_map/cond
